TPU v7x, 32 devices: a whole 2x2x4 slice. The times are simulated.
32 devices in a mesh: groups: 2 (over y), vocab: 4 (over z), edit: 2 (over x), tok: 2 (over core).
Axes of the slice: x: 2, y: 2, z: 4, core: 2. Of those that a mesh axis runs over, the one named last changes fastest.
Arguments:
- token_ids: int32 [256], P(('groups', 'tok')), parts along dimension 0, may hold values from 0 to 4095
- valid_mask: int32 [256], P(('groups', 'tok')), parts along dimension 0, may hold values 0 or 1
- key_index: int32 [4], P('groups'), parts along dimension 0, may hold values from 0 to 3
- hidden_act: bfloat16 [256, 14336], P(('groups', 'tok'), 'vocab'), parts along dimension 0, may hold values from -6 to 6
- key_table: bfloat16 [4, 14336], P(None, 'vocab'), may hold values from -0.046875 to 0.046875
- base_out: bfloat16 [256, 4096], P(('groups', 'tok'), 'vocab'), parts along dimension 0, may hold values from -50 to 50
- value_vecs: bfloat16 [4, 4096], P(('groups', 'edit'), 'vocab'), parts along dimension 0, may hold values from -6 to 6
- norm_gain: float32 [4096], replicated, may hold values from 0.5 to 1.5
- head: bfloat16 [4096, 4096], P(('vocab', 'edit')), may hold values from -46 to 46
Outputs:
- grad_value: float32 [4, 4096], P(('groups', 'edit'), 'vocab'), parts along dimension 0
- token_kl: float32 [4, 128], P(('groups', 'edit'), 'tok'), parts along dimension 0
- target_logprob: float32 [4, 128], P(('groups', 'edit'), 'tok'), parts along dimension 0
There are 2 independent parts, one for each index of `groups`. A program takes and returns all parts, laid end to end along the dimension named above; an argument that names none is the same for every part. Nothing has to cross between parts.
All inputs are finite; a program needn't handle non-finite values. No bound on the sum of `valid_mask` on one device may be relied on, other than what follows from the above.
Results may differ from a plain program's by a relative error of at most 0.0061.
Values may be sent and summed in bfloat16 or wider, within the bound.
A program may use at most 64 MiB of HBM per device.

v0:
```python
import jax
import jax.numpy as jnp
from jax import lax
from jax.sharding import PartitionSpec as P

NORM_EPS = 1e-05


def rms_scale(hidden_rows):
    return lax.rsqrt(jnp.mean(hidden_rows * hidden_rows, axis=-1, keepdims=True) + NORM_EPS)


def per_device(
    token_ids, valid_mask, key_index, hidden_act, key_table, base_out, value_vecs, norm_gain, head
):
    vocab_rows = head.shape[0]
    edit_rows = value_vecs.shape[0]
    piece_width = value_vecs.shape[1]
    key_slots = jnp.arange(key_table.shape[0], dtype=jnp.int32)
    select = (key_index[:, None] == key_slots[None, :]).astype(jnp.bfloat16)
    edit_keys = jnp.dot(select, key_table, preferred_element_type=jnp.float32).astype(jnp.bfloat16)
    coeff_part = lax.dot_general(
        edit_keys, hidden_act, (((1,), (1,)), ((), ())), preferred_element_type=jnp.float32
    )
    coeff = lax.psum(coeff_part, "vocab")
    base_rows, local_values = (
        lax.all_gather(base_out, "vocab", axis=1, tiled=True),
        lax.all_gather(value_vecs, "vocab", axis=1, tiled=True),
    )
    values = lax.all_gather(local_values, "edit", axis=0, tiled=True)
    base32 = base_rows.astype(jnp.float32)
    base_norm = (norm_gain * base32 * rms_scale(base32)).astype(jnp.bfloat16)
    base_logits = lax.dot_general(
        base_norm, head, (((1,), (1,)), ((), ())), preferred_element_type=jnp.float32
    )
    edited = base32[None, :, :] + coeff[:, :, None] * values.astype(jnp.float32)[:, None, :]
    row_scale = rms_scale(edited)
    normed = (norm_gain * edited * row_scale).astype(jnp.bfloat16)
    logits = jnp.einsum("etd,vd->etv", normed, head, preferred_element_type=jnp.float32)
    vocab_start = lax.axis_index(("vocab", "edit")) * vocab_rows
    vocab_ids = vocab_start + jnp.arange(vocab_rows, dtype=jnp.int32)
    onehot = (token_ids[:, None] == vocab_ids[None, :]).astype(jnp.float32)
    peak_base = jnp.max(base_logits, axis=-1)
    peak_edit = jnp.max(logits, axis=-1)
    peak_base, peak_edit = lax.pmax((peak_base, peak_edit), ("vocab", "edit"))
    base_exp = jnp.exp(base_logits - peak_base[:, None])
    base_total = jnp.sum(base_exp, axis=-1)
    edit_total = jnp.sum(jnp.exp(logits - peak_edit[:, :, None]), axis=-1)
    cross_sum = jnp.sum(base_exp[None, :, :] * (base_logits[None, :, :] - logits), axis=-1)
    target = jnp.sum(onehot[None, :, :] * logits, axis=-1)
    base_total, edit_total, cross_sum, target = lax.psum(
        (base_total, edit_total, cross_sum, target), ("vocab", "edit")
    )
    base_lse = peak_base + jnp.log(base_total)
    edit_lse = peak_edit + jnp.log(edit_total)
    valid = valid_mask.astype(jnp.float32)
    token_kl = valid[None, :] * (cross_sum / base_total[None, :] - base_lse[None, :] + edit_lse)
    target_logprob = target - edit_lse
    base_prob = jnp.exp(base_logits - base_lse[:, None])
    edit_prob = jnp.exp(logits - edit_lse[:, :, None])
    logit_grad = (valid[None, :, None] * (edit_prob - base_prob[None, :, :])).astype(jnp.bfloat16)
    back_rows = jnp.einsum("etv,vd->etd", logit_grad, head, preferred_element_type=jnp.float32)
    grad_y = norm_gain * back_rows
    grad_o = row_scale * grad_y - edited * row_scale**3 * jnp.mean(
        grad_y * edited, axis=-1, keepdims=True
    )
    grad_part = jnp.sum(coeff[:, :, None] * grad_o, axis=1)
    edit_start = lax.axis_index("edit") * edit_rows
    grad_total = lax.psum(grad_part, ("vocab", "edit", "tok"))
    grad_mine = lax.dynamic_slice_in_dim(grad_total, edit_start, edit_rows, 0)
    grad_piece = lax.dynamic_slice_in_dim(
        grad_mine, lax.axis_index("vocab") * piece_width, piece_width, 1
    )
    kl_mine = lax.dynamic_slice_in_dim(token_kl, edit_start, edit_rows, 0)
    target_mine = lax.dynamic_slice_in_dim(target_logprob, edit_start, edit_rows, 0)
    return (grad_piece, kl_mine, target_mine)


def solution(mesh):
    placed = (
        P(("groups", "tok")),
        P(("groups", "tok")),
        P("groups"),
        P(("groups", "tok"), "vocab"),
        P(None, "vocab"),
        P(("groups", "tok"), "vocab"),
        P(("groups", "edit"), "vocab"),
        P(),
        P(("vocab", "edit"), None),
    )
    return jax.shard_map(
        per_device,
        mesh=mesh,
        in_specs=placed,
        out_specs=(
            P(("groups", "edit"), "vocab"),
            P(("groups", "edit"), "tok"),
            P(("groups", "edit"), "tok"),
        ),
        check_vma=False,
    )
```

profile of v0, /device:TPU:0, one launch (start us, length us, event | category | flops | bytes accessed | tf_op | source)
XLA Modules:
  0.0 156.0 jit_solution(18408327459742363050)
XLA Ops:
  0.6 0.0 copy-start
  0.7 0.7 convert_element_type.32
  1.4 0.3 copy-done
  1.7 1.1 fusion.3
  2.8 13.4 %psum.42 = f32[2,64]{1,0:T(2,128)S(1)} all-reduce(f32[2,64]{1,0:T(2,128)S(1)} %fusion.3), channel_id=1, replica_groups=mesh['groups'=2,'vocab'=4,'edit'=2,'tok'=2] {'vocab'}, use_global_device_ids=true, to_apply=%region_0.0 | all-reduce | flops 128 | bytes 1024 | tf_op jit(solution)/shard_map/psum | solution.py:25
  16.3 13.3 %all_gather.10 = bf16[1,4096]{1,0:T(2,128)(2,1)S(1)} all-gather(bf16[1,1024]{1,0:T(2,128)(2,1)} %param.15), channel_id=1, replica_groups=mesh['groups'=2,'vocab'=4,'edit'=2,'tok'=2] {'vocab'}, dimensions={1}, use_global_device_ids=true | all-gather | bytes 10240 | tf_op jit(solution)/shard_map/all_gather | solution.py:28
  29.5 4.4 %all-gather = bf16[2,1,4096]{2,1,0:T(2,128)(2,1)S(1)} all-gather(bf16[1,1,4096]{2,1,0:T(2,128)(2,1)S(1)} %bitcast.20), channel_id=1, replica_groups=mesh['groups'=2,'vocab'=4,'edit'=2,'tok'=2] {'edit'}, dimensions={0}, use_global_device_ids=true | all-gather | bytes 24576 | tf_op jit(solution)/shard_map/all_gather | solution.py:30
  34.0 0.7 compare_convert_fusion
  34.7 15.0 %all_gather.9 = bf16[64,4096]{1,0:T(8,128)(2,1)S(1)} all-gather(bf16[64,1024]{1,0:T(8,128)(2,1)} %param.14), channel_id=1, replica_groups=mesh['groups'=2,'vocab'=4,'edit'=2,'tok'=2] {'vocab'}, dimensions={1}, use_global_device_ids=true | all-gather | bytes 655360 | tf_op jit(solution)/shard_map/all_gather | solution.py:27
  49.7 0.2 multiply_reduce_fusion.3
  49.9 0.0 copy-start.1
  49.9 3.9 %fusion.24 = (f32[64]{0:T(128)S(1)}, f32[64,512]{1,0:T(8,128)S(1)}) fusion(bf16[512,4096]{1,0:T(8,128)(2,1)} %param.17, f32[64]{0:T(128)S(1)} %add_rsqrt_fusion.1, f32[4096]{0:T(1024)} %param.16, bf16[64,4096]{1,0:T(8,128)(2,1)S(1)} %all_gather.9), kind=kOutput, calls=%fused_computation.48 | convolution fusion | flops 269516736 | bytes 4866560 | tf_op jit(solution)/shard_map/dot_general | solution.py:33
  53.8 0.0 copy-start.2
  53.8 0.1 convert_element_type.30
  53.9 0.4 multiply_reduce_fusion.2
  54.3 0.0 copy-done.1
  54.3 0.2 copy-done.2
  54.5 1.6 %fusion.25 = (f32[2,64]{1,0:T(2,128)S(1)}, f32[2,64,512]{2,1,0:T(8,128)S(1)}) fusion(bf16[512,4096]{1,0:T(8,128)(2,1)S(1)} %copy-done.1, f32[4096]{0:T(1024)S(1)} %copy-done.2, f32[2,64]{1,0:T(2,128)S(1)} %get-tuple-element.17, f32[2,4096]{1,0:T(2,128)S(1)} %bitcast.17, f32[64,4096]{1,0:T(8,128)S(1)} %convert_element_type.30, f32[2,64]{1,0:T(2,128)S(1)} %psum.42), kind=kOutput, calls=%fused_computation.49 | convolution fusion | flops 539557760 | bytes 5555712 | tf_op jit(solution)/shard_map/etd,vd->etv/dot_general | solution.py:39
  56.1 18.6 %all-reduce.1 = (f32[64]{0:T(128)S(1)}, f32[2,64]{1,0:T(2,128)S(1)}) all-reduce(f32[64]{0:T(128)S(1)} %get-tuple-element.18, f32[2,64]{1,0:T(2,128)S(1)} %get-tuple-element.20), channel_id=1, replica_groups=mesh['groups'=2,'vocab'=4,'edit'=2,'tok'=2] {'vocab','edit'}, use_global_device_ids=true, to_apply=%region_8.0 | all-reduce | flops 192 | bytes 1536 | tf_op jit(solution)/shard_map/pmax | solution.py:45
  74.7 0.2 fusion.23
  74.9 0.2 multiply_reduce_fusion.4
  75.1 17.7 %all-reduce = (f32[64]{0:T(128)S(1)}, f32[2,64]{1,0:T(2,128)S(1)}, f32[2,64]{1,0:T(2,128)S(1)}, f32[2,64]{1,0:T(2,128)S(1)}) all-reduce(f32[64]{0:T(128)S(1)} %get-tuple-element.14, f32[2,64]{1,0:T(2,128)S(1)} %get-tuple-element.5, ...), channel_id=1, replica_groups=mesh['groups'=2,'vocab'=4,'edit'=2,'tok'=2] {'vocab','edit'}, use_global_device_ids=true, to_apply=%region_10.0 | all-reduce | flops 448 | bytes 3584 | tf_op jit(solution)/shard_map/psum | solution.py:51
  92.8 0.1 subtract_exponential_fusion
  92.9 0.5 constant_dynamic-slice_fusion
  93.4 3.4 %multiply_reduce_fusion.1 = (f32[2,64]{1,0:T(2,128)S(1)}, f32[2,64,4096]{2,1,0:T(8,128)S(1)}) fusion(f32[2,4096]{1,0:T(2,128)S(1)} %bitcast.18, f32[64,4096]{1,0:T(8,128)S(1)} %convert_element_type.30, f32[2,64]{1,0:T(2,128)S(1)} %psum.42, bf16[512,4096]{1,0:T(8,128)(2,1)} %param.17, f32[2,64,512]{2,1,0:T(8,128)S(1)} %get-tuple-element.21, ...), kind=kOutput, calls=%fused_computation.6 | convolution fusion | flops 539754368 | bytes 7784192 | tf_op jit(solution)/shard_map/etv,vd->etd/dot_general | solution.py:62
  96.9 0.8 multiply_reduce_fusion
  97.7 57.6 %psum.45 = f32[2,4096]{1,0:T(2,128)S(1)} all-reduce(f32[2,4096]{1,0:T(2,128)S(1)} %multiply_reduce_fusion), channel_id=1, replica_groups=mesh['groups'=2,'vocab'=4,'edit'=2,'tok'=2] {'vocab','edit','tok'}, use_global_device_ids=true, to_apply=%region_13.0 | all-reduce | flops 8192 | bytes 65536 | tf_op jit(solution)/shard_map/psum | solution.py:69
  155.3 0.7 dynamic_slice.10
  (8 shorter events, 0.1 us)
Async XLA Ops:
  0.6 1.0 copy-start
  49.9 4.4 %copy-start.1 = (bf16[512,4096]{1,0:T(8,128)(2,1)S(1)}, bf16[512,4096]{1,0:T(8,128)(2,1)}, u32[]{:S(2)}) copy-start(bf16[512,4096]{1,0:T(8,128)(2,1)} %param.17) | copy-start | bytes 12582916
  53.8 0.7 copy-start.2
where the time goes:
time: 156 us
  blocking collectives  140 us (90%)
  matrix products  10 us (6%)
  other arithmetic  3.51 us (2%)
  local copies, waits for them, and re-layouts  1.73 us (1%)
    psum x1, blocking collectives, per_device(): grad_total = lax.psum(grad_part, ('vocab', 'edit', 'tok'))  57.6 us
    pmax x1, blocking collectives, per_device(): peak_base, peak_edit = lax.pmax((peak_base, peak_edit), ('vocab', 'edit'))  18.6 us
    psum x1, blocking collectives, per_device(): lax.psum((base_total, edit_total, cross_sum, target), ('vocab', 'edit'))  17.7 us
    all_gather x1, blocking collectives, per_device(): lax.all_gather(base_out, 'vocab', axis=1, tiled=True)  15 us
    psum x1, blocking collectives, per_device(): coeff = lax.psum(coeff_part, 'vocab')  13.4 us
    all_gather x1, blocking collectives, per_device(): lax.all_gather(value_vecs, 'vocab', axis=1, tiled=True)  13.3 us
    all_gather x1, blocking collectives, per_device(): values = lax.all_gather(local_values, 'edit', axis=0, tiled=True)  4.4 us
    dot_general x1, matrix products, per_device(): lax.dot_general(base_norm, head, (((1,), (1,)), ((), ())), preferred_elem...  3.87 us

commit v1 on v0

--- a/solution.py
+++ b/solution.py
@@ -66,7 +66,7 @@
     )
     grad_part = jnp.sum(coeff[:, :, None] * grad_o, axis=1)
     edit_start = lax.axis_index("edit") * edit_rows
-    grad_total = lax.psum(grad_part, ("vocab", "edit", "tok"))
+    grad_total = jnp.sum(lax.all_gather(grad_part, ("vocab", "edit", "tok")), axis=0)
     grad_mine = lax.dynamic_slice_in_dim(grad_total, edit_start, edit_rows, 0)
     grad_piece = lax.dynamic_slice_in_dim(
         grad_mine, lax.axis_index("vocab") * piece_width, piece_width, 1

time: 156 us -> 119 us (0.76)
  blocking collectives: 140 us -> 102 us
    psum x1 -> x0, blocking collectives: 57.6 us -> none  [per_device(): grad_total = lax.psum(grad_part, ('vocab', 'edit', 'tok'))]
    all_gather x0 -> x1, blocking collectives: none -> 20 us  [per_device(): lax.all_gather(grad_part, ('vocab', 'edit', 'tok'))]
where the time goes in v1:
time: 119 us
  blocking collectives  102 us (86%)
  matrix products  10 us (8%)
  other arithmetic  3.67 us (3%)
  local copies, waits for them, and re-layouts  1.73 us (1%)
    all_gather x1, blocking collectives, per_device(): lax.all_gather(grad_part, ('vocab', 'edit', 'tok'))  20 us
    pmax x1, blocking collectives, per_device(): peak_base, peak_edit = lax.pmax((peak_base, peak_edit), ('vocab', 'edit'))  18.6 us
    psum x1, blocking collectives, per_device(): lax.psum((base_total, edit_total, cross_sum, target), ('vocab', 'edit'))  17.7 us
    all_gather x1, blocking collectives, per_device(): lax.all_gather(base_out, 'vocab', axis=1, tiled=True)  15 us
    psum x1, blocking collectives, per_device(): coeff = lax.psum(coeff_part, 'vocab')  13.4 us
    all_gather x1, blocking collectives, per_device(): lax.all_gather(value_vecs, 'vocab', axis=1, tiled=True)  13.3 us
    all_gather x1, blocking collectives, per_device(): values = lax.all_gather(local_values, 'edit', axis=0, tiled=True)  4.4 us
    dot_general x1, matrix products, per_device(): lax.dot_general(base_norm, head, (((1,), (1,)), ((), ())), preferred_elem...  3.87 us

profile of v1, /device:TPU:0, one launch (start us, length us, event | category | flops | bytes accessed | tf_op | source)
XLA Modules:
  0.0 118.5 jit_solution(2738051936073402506)
XLA Ops:
  0.6 0.0 copy-start
  0.7 0.7 convert_element_type.32
  1.4 0.3 copy-done
  1.7 1.1 fusion.3
  2.8 13.4 %psum.35 = f32[2,64]{1,0:T(2,128)S(1)} all-reduce(f32[2,64]{1,0:T(2,128)S(1)} %fusion.3), channel_id=1, replica_groups=mesh['groups'=2,'vocab'=4,'edit'=2,'tok'=2] {'vocab'}, use_global_device_ids=true, to_apply=%region_0.0 | all-reduce | flops 128 | bytes 1024 | tf_op jit(solution)/shard_map/psum | solution.py:25
  16.3 13.3 %all_gather.16 = bf16[1,4096]{1,0:T(2,128)(2,1)S(1)} all-gather(bf16[1,1024]{1,0:T(2,128)(2,1)} %param.15), channel_id=1, replica_groups=mesh['groups'=2,'vocab'=4,'edit'=2,'tok'=2] {'vocab'}, dimensions={1}, use_global_device_ids=true | all-gather | bytes 10240 | tf_op jit(solution)/shard_map/all_gather | solution.py:28
  29.5 4.4 %all-gather.1 = bf16[2,1,4096]{2,1,0:T(2,128)(2,1)S(1)} all-gather(bf16[1,1,4096]{2,1,0:T(2,128)(2,1)S(1)} %bitcast.22), channel_id=1, replica_groups=mesh['groups'=2,'vocab'=4,'edit'=2,'tok'=2] {'edit'}, dimensions={0}, use_global_device_ids=true | all-gather | bytes 24576 | tf_op jit(solution)/shard_map/all_gather | solution.py:30
  34.0 0.7 compare_convert_fusion
  34.7 15.0 %all_gather.15 = bf16[64,4096]{1,0:T(8,128)(2,1)S(1)} all-gather(bf16[64,1024]{1,0:T(8,128)(2,1)} %param.14), channel_id=1, replica_groups=mesh['groups'=2,'vocab'=4,'edit'=2,'tok'=2] {'vocab'}, dimensions={1}, use_global_device_ids=true | all-gather | bytes 655360 | tf_op jit(solution)/shard_map/all_gather | solution.py:27
  49.7 0.2 multiply_reduce_fusion.3
  49.9 0.0 copy-start.1
  49.9 3.9 %fusion.24 = (f32[64]{0:T(128)S(1)}, f32[64,512]{1,0:T(8,128)S(1)}) fusion(bf16[512,4096]{1,0:T(8,128)(2,1)} %param.17, f32[64]{0:T(128)S(1)} %add_rsqrt_fusion.1, f32[4096]{0:T(1024)} %param.16, bf16[64,4096]{1,0:T(8,128)(2,1)S(1)} %all_gather.15), kind=kOutput, calls=%fused_computation.48 | convolution fusion | flops 269516736 | bytes 4866560 | tf_op jit(solution)/shard_map/dot_general | solution.py:33
  53.8 0.0 copy-start.2
  53.8 0.1 convert_element_type.30
  53.9 0.4 multiply_reduce_fusion.2
  54.3 0.0 copy-done.1
  54.3 0.2 copy-done.2
  54.5 1.6 %fusion.25 = (f32[2,64]{1,0:T(2,128)S(1)}, f32[2,64,512]{2,1,0:T(8,128)S(1)}) fusion(bf16[512,4096]{1,0:T(8,128)(2,1)S(1)} %copy-done.1, f32[4096]{0:T(1024)S(1)} %copy-done.2, f32[2,64]{1,0:T(2,128)S(1)} %get-tuple-element.17, f32[2,4096]{1,0:T(2,128)S(1)} %bitcast.18, f32[64,4096]{1,0:T(8,128)S(1)} %convert_element_type.30, f32[2,64]{1,0:T(2,128)S(1)} %psum.35), kind=kOutput, calls=%fused_computation.49 | convolution fusion | flops 539557760 | bytes 5555712 | tf_op jit(solution)/shard_map/etd,vd->etv/dot_general | solution.py:39
  56.1 18.6 %all-reduce.1 = (f32[64]{0:T(128)S(1)}, f32[2,64]{1,0:T(2,128)S(1)}) all-reduce(f32[64]{0:T(128)S(1)} %get-tuple-element.18, f32[2,64]{1,0:T(2,128)S(1)} %get-tuple-element.20), channel_id=1, replica_groups=mesh['groups'=2,'vocab'=4,'edit'=2,'tok'=2] {'vocab','edit'}, use_global_device_ids=true, to_apply=%region_8.0 | all-reduce | flops 192 | bytes 1536 | tf_op jit(solution)/shard_map/pmax | solution.py:45
  74.7 0.2 fusion.23
  74.9 0.2 multiply_reduce_fusion.4
  75.1 17.7 %all-reduce = (f32[64]{0:T(128)S(1)}, f32[2,64]{1,0:T(2,128)S(1)}, f32[2,64]{1,0:T(2,128)S(1)}, f32[2,64]{1,0:T(2,128)S(1)}) all-reduce(f32[64]{0:T(128)S(1)} %get-tuple-element.14, f32[2,64]{1,0:T(2,128)S(1)} %get-tuple-element.5, ...), channel_id=1, replica_groups=mesh['groups'=2,'vocab'=4,'edit'=2,'tok'=2] {'vocab','edit'}, use_global_device_ids=true, to_apply=%region_10.0 | all-reduce | flops 448 | bytes 3584 | tf_op jit(solution)/shard_map/psum | solution.py:51
  92.8 0.1 subtract_exponential_fusion
  92.9 0.5 constant_dynamic-slice_fusion
  93.4 3.4 %multiply_reduce_fusion.1 = (f32[2,64]{1,0:T(2,128)S(1)}, f32[2,64,4096]{2,1,0:T(8,128)S(1)}) fusion(f32[2,4096]{1,0:T(2,128)S(1)} %bitcast.19, f32[64,4096]{1,0:T(8,128)S(1)} %convert_element_type.30, f32[2,64]{1,0:T(2,128)S(1)} %psum.35, bf16[512,4096]{1,0:T(8,128)(2,1)} %param.17, f32[2,64,512]{2,1,0:T(8,128)S(1)} %get-tuple-element.21, ...), kind=kOutput, calls=%fused_computation.6 | convolution fusion | flops 539754368 | bytes 7784192 | tf_op jit(solution)/shard_map/etv,vd->etd/dot_general | solution.py:62
  96.9 0.8 multiply_reduce_fusion
  97.7 20.0 %all-gather.2 = f32[16,2,4096]{2,1,0:T(2,128)S(1)} all-gather(f32[1,2,4096]{2,1,0:T(2,128)S(1)} %bitcast.21), channel_id=2, replica_groups=mesh['groups'=2,'vocab'=4,'edit'=2,'tok'=2] {'vocab','edit','tok'}, dimensions={0}, use_global_device_ids=true | all-gather | bytes 557056 | tf_op jit(solution)/shard_map/all_gather | solution.py:69
  117.7 0.2 reduce_sum.87
  117.8 0.7 dynamic_slice.10
  (8 shorter events, 0.1 us)
Async XLA Ops:
  0.6 1.0 copy-start
  49.9 4.4 %copy-start.1 = (bf16[512,4096]{1,0:T(8,128)(2,1)S(1)}, bf16[512,4096]{1,0:T(8,128)(2,1)}, u32[]{:S(2)}) copy-start(bf16[512,4096]{1,0:T(8,128)(2,1)} %param.17) | copy-start | bytes 12582916
  53.8 0.7 copy-start.2
